TPU v7x, 32 devices: a whole 2x2x4 slice. The times are simulated.
32 devices in a mesh: frame: 4 (over y, x), head: 8 (over z, core).
Axes of the slice: x: 2, y: 2, z: 4, core: 2. Of those that a mesh axis runs over, the one named last changes fastest.
Arguments:
- tokens: bfloat16 [4096, 5120], P('frame', 'head'), may hold values from -16 to 16
- qkv_weight: bfloat16 [3, 5120, 2048], P(None, None, 'head'), may hold values from -0.1118034 to 0.1118034
- out_weight: bfloat16 [2048, 5120], P('head'), may hold values from -0.1875 to 0.1875
- modulation: float32 [3, 5120], replicated, may hold values from -3 to 3
- block_mask: int32 [16, 32, 32], P('head', 'frame'), may hold values from 0 to 1, as said below
Outputs:
- mixed: bfloat16 [4096, 5120], P('frame', 'head')
Inputs may be any that keep to these rules, and one draw needn't show every extreme that they name: `block_mask`: 1 keeps a pair of 128-token blocks; every query block keeps its own block.
All inputs are finite; a program needn't handle non-finite values.
Results may differ from a plain program's by a relative error of at most 0.0085.
Values may be sent and summed in bfloat16 or wider, within the bound.
A program may use at most 256 MiB of HBM per device.

v0:
```python
import math

import jax
import jax.numpy as jnp
from jax import lax
from jax.sharding import PartitionSpec as P

BLK = 128


NEGATIVE = -1e30
EPSILON = 1e-06


def update_heads(state, query, keys, values, keep, scale):
    top, total, summed = state
    scores = jnp.einsum("qhd,khd->hqk", query, keys, preferred_element_type=jnp.float32) * scale
    masked = jnp.where(keep, scores, NEGATIVE)
    new_top = jnp.maximum(top, jnp.max(masked, axis=2))
    weights = jnp.where(keep, jnp.exp(scores - new_top[:, :, None]), 0.0)
    total = jnp.sum(weights, axis=2)
    summed = jnp.einsum(
        "hqk,khd->hqd", weights.astype(jnp.bfloat16), values, preferred_element_type=jnp.float32
    )
    return (new_top, total, summed)


def shards(tokens, qkv_weight, out_weight, modulation, block_mask):
    local_rows, local_cols = tokens.shape
    heads_here = block_mask.shape[0]
    inner = qkv_weight.shape[2]
    head_size = inner // heads_here
    scale = 1.0 / math.sqrt(head_size)
    col_start = lax.axis_index("head") * local_cols
    own_mod = lax.dynamic_slice_in_dim(modulation, col_start, local_cols, 1)
    whole = lax.all_gather(tokens, "head", axis=1, tiled=True)
    wide = whole.astype(jnp.float32)
    center = jnp.mean(wide, axis=1, keepdims=True)
    spread = jnp.mean(jnp.square(wide - center), axis=1, keepdims=True)
    normed = (
        (wide - center) * lax.rsqrt(spread + EPSILON) * (1.0 + modulation[1]) + modulation[0]
    ).astype(jnp.bfloat16)
    projected = jnp.einsum("td,jdc->jtc", normed, qkv_weight, preferred_element_type=jnp.float32)
    query = projected[0].astype(jnp.bfloat16).reshape(local_rows, heads_here, head_size)
    keyed = projected[1].astype(jnp.bfloat16)
    valued = projected[2].astype(jnp.bfloat16)
    start_state = (
        jnp.full((heads_here, local_rows), NEGATIVE, jnp.float32),
        jnp.zeros((heads_here, local_rows), jnp.float32),
        jnp.zeros((heads_here, local_rows, head_size), jnp.float32),
    )
    key_piece = lax.all_gather(keyed, "frame", axis=0, tiled=True)
    value_piece = lax.all_gather(valued, "frame", axis=0, tiled=True)
    count = key_piece.shape[0]
    keys = key_piece.reshape(count, heads_here, head_size)
    values = value_piece.reshape(count, heads_here, head_size)
    blocks = block_mask > 0
    keep = jnp.repeat(jnp.repeat(blocks, BLK, axis=1), BLK, axis=2)
    top, total, summed = update_heads(start_state, query, keys, values, keep, scale)
    heads_done = (
        (summed / total[:, :, None])
        .astype(jnp.bfloat16)
        .transpose(1, 0, 2)
        .reshape(local_rows, inner)
    )
    mixed_cols = lax.psum_scatter(
        lax.dot_general(
            out_weight, heads_done, (((0,), (1,)), ((), ())), preferred_element_type=jnp.float32
        ).astype(jnp.bfloat16),
        "head",
        scatter_dimension=0,
        tiled=True,
    ).astype(jnp.float32)
    mixed = mixed_cols.T
    return (tokens.astype(jnp.float32) + own_mod[2] * mixed).astype(jnp.bfloat16)


def solution(mesh):
    placed = (
        P("frame", "head"),
        P(None, None, "head"),
        P("head", None),
        P(),
        P("head", "frame", None),
    )
    return jax.shard_map(
        shards, mesh=mesh, in_specs=placed, out_specs=P("frame", "head"), check_vma=False
    )
```

profile of v0, /device:TPU:1, one launch (start us, length us, event | category | flops | bytes accessed | tf_op | source)
XLA Modules:
  0.0 364.2 jit_solution(10629822894441542504)
XLA Ops:
  6.5 0.7 all-gather.6.cloned.1.call-update
  7.3 0.0 all-gather.8.cloned.1.call-start
  7.3 1.0 slice_add_fusion
  8.3 102.5 %all-gather.6.cloned.1.call-done = bf16[1024,5120]{1,0:T(8,128)(2,1)} async-done(((bf16[1024,640]{1,0:T(8,128)(2,1)}), bf16[1024,5120]{1,0:T(8,128)(2,1)}) %all-gather.6.cloned.1.call-update) | async-done | bytes 10485776 | tf_op jit(solution)/shard_map/all_gather | solution.py:36
  110.8 5.4 %convert_reduce_fusion = f32[1024]{0:T(1024)S(1)} fusion(bf16[1024,5120]{1,0:T(8,128)(2,1)} %all-gather.6.cloned.1.call-done), kind=kLoop, calls=%fused_computation.3 | loop fusion | flops 10484736 | bytes 10489856 | tf_op jit(solution)/shard_map/reduce_sum | solution.py:38
  116.2 6.8 %fusion.4 = f32[1024]{0:T(1024)S(1)} fusion(bf16[1024,5120]{1,0:T(8,128)(2,1)} %all-gather.6.cloned.1.call-done, f32[1024]{0:T(1024)S(1)} %broadcast_multiply_fusion), kind=kLoop, calls=%fused_computation.8 | loop fusion | flops 20970496 | bytes 10493952 | tf_op jit(solution)/shard_map/reduce_sum | solution.py:39
  123.1 13.9 %fusion.17 = bf16[3,1024,256]{1,2,0:T(8,128)(2,1)S(1)} fusion(bf16[3,5120,256]{2,1,0:T(8,128)(2,1)} %param.6, bf16[1024,5120]{1,0:T(8,128)(2,1)} %all-gather.6.cloned.1.call-done, f32[5120]{0:T(1024)S(1)} %bitcast.41, f32[5120]{0:T(1024)S(1)} %bitcast.40, f32[1024]{0:T(1024)S(1)} %add_rsqrt_fusion, f32[1024]{0:T(1024)S(1)} %broadcast_multiply_fusion), kind=kOutput, calls=%fused_computation.19 | convolution fusion | flops 8085307392 | bytes 19972096 | tf_op jit(solution)/shard_map/td,jdc->jtc/dot_general | solution.py:43
  137.0 1.1 fusion.27
  138.1 0.0 all-gather.10.cloned.1.call-start
  138.2 0.1 broadcast_in_dim.21
  138.3 12.2 %broadcast_in_dim.22 = pred[2,1024,32,128]{3,2,1,0:T(32,128)(4,1)} broadcast(pred[2,1024,32]{2,1,0:T(8,128)(4,1)S(1)} %bitcast.38), dimensions={0,1,2} | broadcast | bytes 8454144 | tf_op jit(solution)/shard_map/broadcast_in_dim | solution.py:58
  150.5 22.8 %reshape.37 = pred[2,1024,4096]{2,1,0:T(32,128)(4,1)} reshape(pred[2,1024,32,128]{3,2,1,0:T(32,128)(4,1)} %broadcast_in_dim.22) | data formatting | bytes 16777216 | tf_op jit(solution)/shard_map/reshape | solution.py:58
  173.4 0.2 reduce-scatter.4.cloned.1.call-start
  173.6 0.0 all-gather.8.cloned.1.call-done
  173.6 17.6 %select_reduce_fusion = (f32[2,1024]{1,0:T(2,128)S(1)}, f32[2,1024,4096]{2,1,0:T(8,128)}) fusion(pred[2,1024,4096]{2,1,0:T(32,128)(4,1)} %reshape.37, bf16[1024,2,128]{0,2,1:T(8,128)(2,1)S(1)} %bitcast.36, bf16[4096,2,128]{0,2,1:T(8,128)(2,1)} %bitcast.37), kind=kOutput, calls=%fused_computation.1 | convolution fusion | flops 2172647424 | bytes 44572672 | tf_op jit(solution)/shard_map/qhd,khd->hqk/dot_general | solution.py:17
  191.3 17.3 %fusion.2 = f32[2,1024]{1,0:T(2,128)S(1)} fusion(pred[2,1024,4096]{2,1,0:T(32,128)(4,1)} %reshape.37, f32[2,1024,4096]{2,1,0:T(8,128)} %get-tuple-element.11, f32[2,1024]{1,0:T(2,128)S(1)} %broadcast_maximum_fusion), kind=kLoop, calls=%fused_computation.6 | loop fusion | flops 33552384 | bytes 41959424 | tf_op jit(solution)/shard_map/reduce_sum | solution.py:21
  208.5 0.0 all-gather.10.cloned.1.call-done
  208.5 16.1 %divide_convert_fusion = bf16[1024,2,128]{0,2,1:T(8,128)(2,1)S(1)} fusion(bf16[4096,2,128]{0,2,1:T(8,128)(2,1)} %bitcast.43, pred[2,1024,4096]{2,1,0:T(32,128)(4,1)} %reshape.37, f32[2,1024,4096]{2,1,0:T(8,128)} %get-tuple-element.11, f32[2,1024]{1,0:T(2,128)S(1)} %broadcast_maximum_fusion, f32[1024,2]{0,1:T(2,128)S(1)} %bitcast.42), kind=kOutput, calls=%fused_computation.21 | convolution fusion | flops 2181562368 | bytes 44580864 | tf_op jit(solution)/shard_map/hqk,khd->hqd/dot_general | solution.py:22
  224.6 5.5 %convert_bitcast_fusion = bf16[5120,1024]{0,1:T(8,128)(2,1)} fusion(bf16[1024,256]{0,1:T(8,128)(2,1)S(1)} %bitcast.39, bf16[256,5120]{1,0:T(8,128)(2,1)S(1)} %copy-done), kind=kOutput, calls=%fused_computation.14 | convolution fusion | flops 2689597440 | bytes 13631488 | tf_op jit(solution)/shard_map/dot_general | solution.py:67
  230.1 14.4 %copy.15 = bf16[5120,1024]{1,0:T(8,128)(2,1)} copy(bf16[5120,1024]{0,1:T(8,128)(2,1)} %convert_bitcast_fusion) | data formatting | bytes 20971520
  244.6 0.8 dynamic-slice_reduce_fusion
  245.4 106.7 %reduce-scatter.4.cloned.1.call-done = bf16[640,1024]{1,0:T(8,128)(2,1)} async-done(((bf16[5120,1024]{1,0:T(8,128)(2,1)}), bf16[640,1024]{1,0:T(8,128)(2,1)}) %reduce-scatter.4.cloned.1.call-update) | async-done | bytes 1310736
  352.1 2.4 copy.16
  354.5 3.2 fusion.13
  (12 shorter events, 0.1 us)
Async XLA Ops:
  6.5 218.1 %copy-start = (bf16[256,5120]{1,0:T(8,128)(2,1)S(1)}, bf16[256,5120]{1,0:T(8,128)(2,1)}, u32[]{:S(2)}) copy-start(bf16[256,5120]{1,0:T(8,128)(2,1)} %param.7) | copy-start | bytes 7864324
  6.5 104.2 %all-gather.6.cloned.1.call-start = ((), (), s32[]{:S(2)}) async-start(), calls=%async_computation.1 | async-start | bytes 11796480 | tf_op jit(solution)/shard_map/all_gather | solution.py:36
  7.3 166.4 %all-gather.8.cloned.1.call-start = ((), (), s32[]{:S(2)}) async-start(), calls=%async_computation.2 | async-start | bytes 2621440 | tf_op jit(solution)/shard_map/all_gather | solution.py:52
  123.0 15.1 %copy-start.1 = (s32[2,8,32]{2,1,0:T(8,128)S(1)}, s32[2,8,32]{2,1,0:T(8,128)}, u32[]{:S(2)}) copy-start(s32[2,8,32]{2,1,0:T(8,128)} %param.9) | copy-start | bytes 6148
  138.1 70.4 %all-gather.10.cloned.1.call-start = ((), (), s32[]{:S(2)}) async-start(), calls=%async_computation.3 | async-start | bytes 2621440 | tf_op jit(solution)/shard_map/all_gather | solution.py:53
  173.4 178.7 %reduce-scatter.4.cloned.1.call-start = ((), (), s32[]{:S(2)}) async-start(), calls=%async_computation.4 | async-start | bytes 11796480
Sparse Core Ops, SparseCore 0:
  8.9 101.7 all-gather.5
  138.2 32.9 all-gather.7
  173.5 34.7 all-gather.9
  244.7 107.3 reduce-scatter.3
where the time goes:
time: 368 us; the launch traced here: 364 us
  waiting for transfers between devices  210 us (57%)
  local copies, waits for them, and re-layouts  53.9 us (15%)
  matrix products  53.1 us (14%)
  other arithmetic  33.7 us (9%)
  between operations  13.2 us (4%)
    unnamed x5, waiting for transfers between devices  107 us
    all_gather x1, waiting for transfers between devices, shards(): whole = lax.all_gather(tokens, 'head', axis=1, tiled=True)  102 us
    reshape x1, local copies, waits for them, and re-layouts, shards(): keep = jnp.repeat(jnp.repeat(blocks, BLK, axis=1), BLK, axis=2)  22.8 us
    dot_general x1, matrix products, update_heads(): jnp.einsum('qhd,khd->hqk', query, keys, preferred_element_type=jnp.float32)  17.6 us
    reduce_sum x1, other arithmetic, update_heads(): total = jnp.sum(weights, axis=2)  17.3 us
    unnamed x6, local copies, waits for them, and re-layouts  16.8 us
    dot_general x1, matrix products, update_heads(): jnp.einsum('hqk,khd->hqd', weights.astype(jnp.bfloat16), values, preferre...  16.1 us
    dot_general x1, matrix products, shards(): jnp.einsum('td,jdc->jtc', normed, qkv_weight, preferred_element_type=jnp....  13.9 us
  transfers between devices with their start and end apart: 4, of which 2 were waited for; matrix products, arithmetic and copies ran while one was open for 20% of the time, Pallas kernels for 0%

commit v1 on v0

v1 whole, which is shorter than its diff:
```python
import functools
import math

import jax
import jax.numpy as jnp
from jax import lax
from jax.experimental import pallas as pl
from jax.experimental.pallas import tpu as pltpu
from jax.sharding import PartitionSpec as P

BLK = 128
NEGATIVE = -1e30
EPSILON = 1e-06
LOG2E = math.log2(math.e)
TOKEN_CHUNKS = 8
QUERY_CHUNKS = 4


def source_of(me, size, step):
    if size & (size - 1) == 0:
        return lax.bitwise_xor(me, step)
    return lax.rem(me + size - step, size)


def target_of(me, size, step):
    if size & (size - 1) == 0:
        return lax.bitwise_xor(me, step)
    return lax.rem(me + step, size)


def chain(me, size):
    return me // 2, me % 2, me + 1 - 2 * (me % 2)


def send(src, dst, send_sem, recv_sem, **where):
    return pltpu.make_async_remote_copy(
        src_ref=src,
        dst_ref=dst,
        send_sem=send_sem,
        recv_sem=recv_sem,
        device_id=where,
        device_id_type=pl.DeviceIdType.MESH,
    )


class Relay:
    def __init__(self, me, size, buffer, span, sems):
        self.me, self.size, self.buffer, self.span = me, size, buffer, span
        self.spot, self.core, self.other = chain(me, size)
        self.line = size // 2
        self.far_send, self.far_recv, self.pair_send, self.pair_recv = sems

    def rows(self, block, chunk):
        start = pl.multiple_of(chunk * self.span, self.span)
        return self.buffer.at[block, pl.ds(start, self.span), :]

    def hop(self, block, chunk, away, source=None):
        ref = self.rows(block, chunk)
        slot = 0 if away > 0 else 1
        return send(
            ref if source is None else source,
            ref,
            self.far_send.at[block // 2, chunk, slot],
            self.far_recv.at[block // 2, chunk],
            head=self.me + 2 * away,
        )

    def pair(self, block, chunk, source=None):
        ref = self.rows(block, chunk)
        return send(
            ref if source is None else source,
            ref,
            self.pair_send.at[block // 2, chunk],
            self.pair_recv.at[block // 2, chunk],
            head=self.other,
        )

    def own(self, chunk, source=None):
        for away in (1, -1):
            edge = self.spot < self.line - 1 if away > 0 else self.spot > 0

            @pl.when(edge)
            def _():
                self.hop(self.me, chunk, away, source).start()

        self.pair(self.me, chunk, source).start()

    def pass_on(self, chunk, distance):
        for away in (1, -1):
            spot = self.spot - away * distance
            here = spot >= 0 if away > 0 else spot < self.line
            edge = self.spot < self.line - 1 if away > 0 else self.spot > 0
            block = spot * 2 + self.core

            @pl.when(here)
            def _():
                self.hop(block, chunk, away).wait_recv()

                @pl.when(edge)
                def _():
                    self.hop(block, chunk, away).start()

                self.pair(block, chunk).start()

    def collect(self, chunk):
        for spot in range(self.line):
            self.pair(spot * 2 + 1 - self.core, chunk).wait_recv()

    def drain(self, chunk):
        for spot in range(self.line):
            block = spot * 2 + self.core
            self.pair(block, chunk).wait_send()
            for away in (1, -1):
                came = spot <= self.spot if away > 0 else spot >= self.spot
                edge = self.spot < self.line - 1 if away > 0 else self.spot > 0

                @pl.when(jnp.logical_and(came, edge))
                def _():
                    self.hop(block, chunk, away).wait_send()


def greet(me, frame, heads_axis, frames):
    barrier = pltpu.get_barrier_semaphore()
    for s in range(1, frames):
        pl.semaphore_signal(
            barrier, inc=1, device_id={"frame": target_of(frame, frames, s)},
            device_id_type=pl.DeviceIdType.MESH,
        )
    for s in range(1, heads_axis):
        pl.semaphore_signal(
            barrier, inc=1, device_id={"head": target_of(me, heads_axis, s)},
            device_id_type=pl.DeviceIdType.MESH,
        )
    pl.semaphore_wait(barrier, frames + heads_axis - 2)


def gather_kernel(
    frames, heads_axis, count, tokens, shift, gain, weight, q_ref, kv_ref,
    got, held, far_send, far_recv, pair_send, pair_recv, kv_send, kv_recv, local,
):
    me, frame = lax.axis_index("head"), lax.axis_index("frame")
    rows, cols = tokens.shape
    span = rows // count
    inner = q_ref.shape[1]
    width = cols * heads_axis
    load = pltpu.make_async_copy(weight, held, local.at[0])
    load.start()
    mine = pltpu.make_async_copy(tokens, got.at[me], local.at[1])
    mine.start()
    greet(me, frame, heads_axis, frames)
    relay = Relay(me, heads_axis, got, span, (far_send, far_recv, pair_send, pair_recv))

    def begin(chunk, carry):
        start = pl.multiple_of(chunk * span, span)
        relay.own(chunk, tokens.at[pl.ds(start, span), :])
        return carry

    lax.fori_loop(0, count, begin, 0)
    mine.wait()
    load.wait()

    def to_frame(chunk, s):
        start = pl.multiple_of(chunk * span, span)
        return send(
            kv_ref.at[0, :, pl.ds(start, span), :],
            kv_ref.at[s, :, pl.ds(start, span), :],
            kv_send.at[chunk, s],
            kv_recv.at[chunk, s],
            frame=target_of(frame, frames, s),
        )

    def step(chunk, carry):
        for distance in range(1, heads_axis // 2):
            relay.pass_on(chunk, distance)
        relay.collect(chunk)
        start = pl.multiple_of(chunk * span, span)
        window = pl.ds(start, span)
        total = jnp.zeros((span, cols), jnp.float32)
        for i in range(heads_axis):
            total += got[i, window, :].astype(jnp.float32)
        center = jnp.sum(total, axis=1, keepdims=True) / width
        square = jnp.zeros((span, cols), jnp.float32)
        for i in range(heads_axis):
            off = got[i, window, :].astype(jnp.float32) - center
            square += off * off
        inverse = lax.rsqrt(jnp.sum(square, axis=1, keepdims=True) / width + EPSILON)
        sums = [jnp.zeros((span, inner), jnp.float32) for _ in range(3)]
        for i in range(heads_axis):
            wide = got[i, window, :].astype(jnp.float32)
            normed = ((wide - center) * inverse * (1.0 + gain[i]) + shift[i]).astype(jnp.bfloat16)
            for j in range(3):
                sums[j] += jnp.dot(
                    normed, held[j, i * cols : (i + 1) * cols, :],
                    preferred_element_type=jnp.float32,
                )
        q_ref[window, :] = sums[0].astype(q_ref.dtype)
        kv_ref[0, 0, window, :] = sums[1].astype(kv_ref.dtype)
        kv_ref[0, 1, window, :] = sums[2].astype(kv_ref.dtype)
        for s in range(1, frames):
            to_frame(chunk, s).start()
        return carry

    lax.fori_loop(0, count, step, 0)

    def finish(chunk, carry):
        relay.drain(chunk)
        for s in range(1, frames):
            to_frame(chunk, s).wait()
        return carry

    lax.fori_loop(0, count, finish, 0)


def gather_project(frames, heads_axis, tokens, shift, gain, weight):
    rows, cols = tokens.shape
    inner = weight.shape[2]
    count = TOKEN_CHUNKS
    line = heads_axis // 2
    whole = pl.BlockSpec(memory_space=pltpu.VMEM)
    away = pl.BlockSpec(memory_space=pl.ANY)
    sem = pltpu.SemaphoreType.DMA
    return pl.pallas_call(
        functools.partial(gather_kernel, frames, heads_axis, count),
        in_specs=[away, whole, whole, away],
        out_specs=[whole, whole],
        out_shape=[
            jax.ShapeDtypeStruct((rows, inner), jnp.bfloat16),
            jax.ShapeDtypeStruct((frames, 2, rows, inner), jnp.bfloat16),
        ],
        scratch_shapes=[
            pltpu.VMEM((heads_axis, rows, cols), jnp.bfloat16),
            pltpu.VMEM(weight.shape, jnp.bfloat16),
            sem((line, count, 2)),
            sem((line, count)),
            sem((line, count)),
            sem((line, count)),
            sem((count, frames)),
            sem((count, frames)),
            sem((2,)),
        ],
        compiler_params=pltpu.CompilerParams(collective_id=0, has_side_effects=True),
        name="gather_project",
    )(tokens, shift, gain, weight)


def attend_kernel(
    frames, heads_axis, heads, count, w_slice, q_ref, kv_ref, bias_ref, weight, tokens, gate,
    out_ref, done, full, far_send, far_recv, pair_send, pair_recv, w_send, w_recv, x_send,
    x_recv, local,
):
    me, frame = lax.axis_index("head"), lax.axis_index("frame")
    rows, inner = q_ref.shape
    head_size = inner // heads
    factor = LOG2E / math.sqrt(head_size)
    span = rows // count
    share = inner // frames
    greet(me, frame, heads_axis, frames)
    relay = Relay(me, heads_axis, done, span, (far_send, far_recv, pair_send, pair_recv))
    band = pl.ds(pl.multiple_of(frame * share, share), share)

    def to_head(s):
        there = target_of(me, heads_axis, s)
        return send(
            w_slice(weight, band, there), full.at[me, band, :], w_send.at[s], w_recv.at[s],
            head=there,
        )

    keep = pltpu.make_async_copy(w_slice(weight, band, me), full.at[me, band, :], local.at[0])
    keep.start()
    for s in range(1, heads_axis):
        to_head(s).start()

    def to_frame(s):
        return send(
            full.at[:, band, :], full.at[:, band, :], x_send.at[s], x_recv.at[s],
            frame=target_of(frame, frames, s),
        )

    def from_frame(s):
        there = source_of(frame, frames, s)
        part = pl.ds(pl.multiple_of(there * share, share), share)
        return send(
            full.at[:, part, :], full.at[:, part, :], x_send.at[s], x_recv.at[s],
            frame=target_of(frame, frames, s),
        )

    def from_head(s):
        there = source_of(me, heads_axis, s)
        ref = full.at[there, band, :]
        return send(ref, ref, w_send.at[s], w_recv.at[s], head=target_of(me, heads_axis, s))

    def tile(t, carry):
        window = pl.ds(pl.multiple_of(t * span, span), span)
        for h in range(heads):
            lanes = slice(h * head_size, (h + 1) * head_size)
            query = q_ref[window, lanes]
            top = jnp.full((1, span), NEGATIVE, jnp.float32)
            total = jnp.zeros((1, span), jnp.float32)
            summed = jnp.zeros((head_size, span), jnp.float32)
            for slot in range(frames):
                scores = lax.dot_general(
                    kv_ref[slot, 0, :, lanes], query, (((1,), (1,)), ((), ())),
                    preferred_element_type=jnp.float32,
                )
                pieces = []
                new_top = top
                for block in range(rows // BLK):
                    row = bias_ref[h, slot, block : block + 1, window]
                    part = scores[block * BLK : (block + 1) * BLK] * factor + row
                    new_top = jnp.maximum(new_top, jnp.max(part, axis=0, keepdims=True))
                    pieces.append(part)
                fade = jnp.exp2(top - new_top)
                total = total * fade
                weights = [jnp.exp2(p - new_top) for p in pieces]
                for w in weights:
                    total += jnp.sum(w, axis=0, keepdims=True)
                joined = jnp.concatenate([w.astype(jnp.bfloat16) for w in weights], axis=0)
                summed = summed * fade + lax.dot_general(
                    kv_ref[slot, 1, :, lanes], joined, (((0,), (0,)), ((), ())),
                    preferred_element_type=jnp.float32,
                )
                top = new_top
            done[me, window, lanes] = (summed / total).T.astype(done.dtype)

        relay.own(t)

        @pl.when(t >= 1)
        def _():
            relay.pass_on(t - 1, 1)

        @pl.when(t == count // 2)
        def _():
            keep.wait()
            for s in range(1, heads_axis):
                from_head(s).wait_recv()
            for s in range(1, frames):
                to_frame(s).start()

        return carry

    lax.fori_loop(0, count, tile, 0)

    def mix(t, carry):
        @pl.when(t == count - 1)
        def _():
            relay.pass_on(t, 1)

        for distance in range(2, heads_axis // 2):
            relay.pass_on(t, distance)
        relay.collect(t)

        @pl.when(t == 0)
        def _():
            for s in range(1, frames):
                from_frame(s).wait_recv()

        window = pl.ds(pl.multiple_of(t * span, span), span)
        total = jnp.zeros(tokens[window, :].shape, jnp.float32)
        for i in range(heads_axis):
            total += jnp.dot(done[i, window, :], full[i], preferred_element_type=jnp.float32)
        wide = tokens[window, :].astype(jnp.float32)
        out_ref[window, :] = (wide + gate[...] * total).astype(out_ref.dtype)
        return carry

    lax.fori_loop(0, count, mix, 0)

    def finish(t, carry):
        relay.drain(t)
        return carry

    lax.fori_loop(0, count, finish, 0)
    for s in range(1, heads_axis):
        to_head(s).wait_send()
    for s in range(1, frames):
        to_frame(s).wait_send()


def attend_mix(frames, heads_axis, heads, query, pairs, bias, out_weight, tokens, gate):
    rows, inner = query.shape
    cols = tokens.shape[1]
    count = QUERY_CHUNKS
    line = heads_axis // 2
    whole = pl.BlockSpec(memory_space=pltpu.VMEM)
    away = pl.BlockSpec(memory_space=pl.ANY)
    sem = pltpu.SemaphoreType.DMA
    if cols % 128 == 0:
        def w_slice(ref, band, there):
            return ref.at[band, pl.ds(pl.multiple_of(there * cols, cols), cols)]
    else:
        out_weight = out_weight.reshape(inner, heads_axis, cols).transpose(1, 0, 2)

        def w_slice(ref, band, there):
            return ref.at[there, band, :]

    return pl.pallas_call(
        functools.partial(attend_kernel, frames, heads_axis, heads, count, w_slice),
        in_specs=[whole, whole, whole, away, whole, whole],
        out_specs=whole,
        out_shape=jax.ShapeDtypeStruct((rows, cols), jnp.bfloat16),
        scratch_shapes=[
            pltpu.VMEM((heads_axis, rows, inner), jnp.bfloat16),
            pltpu.VMEM((heads_axis, inner, cols), jnp.bfloat16),
            sem((line, count, 2)),
            sem((line, count)),
            sem((line, count)),
            sem((line, count)),
            sem((heads_axis,)),
            sem((heads_axis,)),
            sem((frames,)),
            sem((frames,)),
            sem((1,)),
        ],
        compiler_params=pltpu.CompilerParams(collective_id=1, has_side_effects=True),
        name="attend_mix",
    )(query, pairs, bias, out_weight, tokens, gate)


def shards(frames, heads_axis, tokens, qkv_weight, out_weight, modulation, block_mask):
    local_rows, local_cols = tokens.shape
    heads_here = block_mask.shape[0]
    head = lax.axis_index("head")
    frame = lax.axis_index("frame")
    shift = modulation[0].reshape(heads_axis, 1, local_cols)
    gain = modulation[1].reshape(heads_axis, 1, local_cols)
    gate = lax.dynamic_slice_in_dim(modulation[2:3], head * local_cols, local_cols, 1)

    per_frame = local_rows // BLK
    bias = jnp.where(block_mask > 0, 0.0, NEGATIVE).astype(jnp.float32)
    bias = jnp.stack(
        [
            lax.dynamic_slice_in_dim(bias, source_of(frame, frames, s) * per_frame, per_frame, 2)
            for s in range(frames)
        ],
        axis=1,
    )
    bias = jnp.repeat(bias.transpose(0, 1, 3, 2), BLK, axis=3)
    query, pairs = gather_project(frames, heads_axis, tokens, shift, gain, qkv_weight)
    return attend_mix(
        frames, heads_axis, heads_here, query, pairs, bias, out_weight, tokens, gate
    )


def solution(mesh):
    placed = (
        P("frame", "head"),
        P(None, None, "head"),
        P("head", None),
        P(),
        P("head", "frame", None),
    )
    body = functools.partial(shards, mesh.shape["frame"], mesh.shape["head"])
    return jax.shard_map(
        body, mesh=mesh, in_specs=placed, out_specs=P("frame", "head"), check_vma=False
    )
```

time: 368 us -> 202 us (0.55); the launches traced: 364 us -> 202 us
  waiting for transfers between devices: 210 us -> 0 us
  Pallas kernels: 0 us -> 196 us
  matrix products: 53.1 us -> 0 us
  local copies, waits for them, and re-layouts: 53.9 us -> 4.87 us
  other arithmetic: 33.7 us -> 1.54 us
  between operations: 13.2 us -> 0.02 us
    pallas_call x0 -> x2, Pallas kernels: none -> 196 us  [the longest x1 120 us: gather_project(): pl.pallas_call(functools.partial(gather_kernel, frames, heads_axis, count...]
    unnamed x5 -> x0, waiting for transfers between devices: 107 us -> none
    all_gather x3 -> x0, waiting for transfers between devices: 103 us -> none  [the longest x1 102 us: shards(): whole = lax.all_gather(tokens, 'head', axis=1, tiled=True)]
    dot_general x4 -> x0, matrix products: 53.1 us -> none  [the longest x1 17.6 us: update_heads(): jnp.einsum('qhd,khd->hqk', query, keys, preferred_element_type=jnp.float32)]
    reduce_sum x3 -> x0, other arithmetic: 29.5 us -> none  [the longest x1 17.3 us: update_heads(): total = jnp.sum(weights, axis=2)]
    reshape x1 -> x0, local copies, waits for them, and re-layouts: 22.8 us -> none  [shards(): keep = jnp.repeat(jnp.repeat(blocks, BLK, axis=1), BLK, axis=2)]
    unnamed x6 -> x1, local copies, waits for them, and re-layouts: 16.8 us -> 2.49 us
    broadcast_in_dim x2 -> x0, local copies, waits for them, and re-layouts: 12.3 us -> none  [shards(): keep = jnp.repeat(jnp.repeat(blocks, BLK, axis=1), BLK, axis=2)]
  transfers between devices with their start and end apart: 4 -> 0, of which waited for: 2 -> 0; matrix products, arithmetic and copies ran while one was open for 20% -> 0% of each run, Pallas kernels for 0% -> 0%
where the time goes in v1:
time: 202 us
  Pallas kernels  196 us (97%)
  local copies, waits for them, and re-layouts  4.87 us (2%)
    pallas_call x1, Pallas kernels, gather_project(): pl.pallas_call(functools.partial(gather_kernel, frames, heads_axis, count...  120 us
    pallas_call x1, Pallas kernels, attend_mix(): pl.pallas_call(functools.partial(attend_kernel, frames, heads_axis, heads...  76 us

profile of v1, /device:TPU:1, one launch (start us, length us, event | category | flops | bytes accessed | tf_op | source)
XLA Modules:
  0.0 202.2 jit_solution(13822829858277170727)
XLA Ops:
  0.0 0.7 compare_select_fusion
  0.7 0.1 dynamic-slice_bitcast_fusion.3
  0.8 1.7 fusion
  2.5 0.6 constant_dynamic-slice_fusion.gate
  3.1 0.8 broadcast_bitcast_fusion.bias_ref
  3.9 119.7 %gather_project.1 = (bf16[1024,256]{1,0:T(8,128)(2,1)}, bf16[4,2,1024,256]{3,2,1,0:T(8,128)(2,1)}) custom-call(bf16[1024,640]{1,0:T(8,128)(2,1)} %tokens.3, f32[8,1,640]{2,1,0:T(1,128)} %bitcast.16, f32[8,1,640]{2,1,0:T(1,128)} %bitcast.17, bf16[3,5120,256]{2,1,0:T(8,128)(2,1)} %weight.2), custom_call_target="tpu_custom_call" | custom-call | tf_op jit(solution)/shard_map/gather_project/pallas_call | solution.py:222
  123.7 76.0 %attend_mix.1 = bf16[1024,640]{1,0:T(8,128)(2,1)} custom-call(bf16[1024,256]{1,0:T(8,128)(2,1)} %get-tuple-element.7.q_ref, bf16[4,2,1024,256]{3,2,1,0:T(8,128)(2,1)} %get-tuple-element.8.kv_ref, f32[2,4,8,1024]{3,2,1,0:T(8,128)} %broadcast_bitcast_fusion.bias_ref, bf16[256,5120]{1,0:T(8,128)(2,1)} %weight.3, bf16[1024,640]{1,0:T(8,128)(2,1)} %tokens.3, ...), custom_call_target="tpu_custom_call" | custom-call | tf_op jit(solution)/shard_map/attend_mix/pallas_call | solution.py:395
  199.7 2.5 %copy.10 = bf16[1024,640]{1,0:T(8,128)(2,1)} copy(bf16[1024,640]{1,0:T(8,128)(2,1)} %attend_mix.1) | data formatting | bytes 2621440

commit v2 on v1

--- a/solution.py
+++ b/solution.py
@@ -102,6 +102,14 @@
 
                 self.pair(block, chunk).start()
 
+    def advance(self, turn, count):
+        for distance in range(1, self.line):
+            chunk = turn - (distance - 1)
+
+            @pl.when(jnp.logical_and(chunk >= 0, chunk < count))
+            def _():
+                self.pass_on(chunk, distance)
+
     def collect(self, chunk):
         for spot in range(self.line):
             self.pair(spot * 2 + 1 - self.core, chunk).wait_recv()
@@ -132,6 +140,20 @@
             device_id_type=pl.DeviceIdType.MESH,
         )
     pl.semaphore_wait(barrier, frames + heads_axis - 2)
+
+
+def contract(parts, weight):
+    cols = parts[0].shape[1]
+    if cols % 128 == 0:
+        return jnp.dot(
+            jnp.concatenate(parts, axis=1), weight, preferred_element_type=jnp.float32
+        )
+    total = 0.0
+    for i, part in enumerate(parts):
+        total += jnp.dot(
+            part, weight[i * cols : (i + 1) * cols], preferred_element_type=jnp.float32
+        )
+    return total
 
 
 def gather_kernel(
@@ -169,9 +191,18 @@
             frame=target_of(frame, frames, s),
         )
 
-    def step(chunk, carry):
-        for distance in range(1, heads_axis // 2):
-            relay.pass_on(chunk, distance)
+    late = max(heads_axis // 2 - 2, 0)
+
+    def turn(i, carry):
+        relay.advance(i, count)
+
+        @pl.when(i >= late)
+        def _():
+            step(i - late)
+
+        return carry
+
+    def step(chunk):
         relay.collect(chunk)
         start = pl.multiple_of(chunk * span, span)
         window = pl.ds(start, span)
@@ -184,23 +215,20 @@
             off = got[i, window, :].astype(jnp.float32) - center
             square += off * off
         inverse = lax.rsqrt(jnp.sum(square, axis=1, keepdims=True) / width + EPSILON)
-        sums = [jnp.zeros((span, inner), jnp.float32) for _ in range(3)]
+        parts = []
         for i in range(heads_axis):
             wide = got[i, window, :].astype(jnp.float32)
-            normed = ((wide - center) * inverse * (1.0 + gain[i]) + shift[i]).astype(jnp.bfloat16)
-            for j in range(3):
-                sums[j] += jnp.dot(
-                    normed, held[j, i * cols : (i + 1) * cols, :],
-                    preferred_element_type=jnp.float32,
-                )
+            parts.append(
+                ((wide - center) * inverse * (1.0 + gain[i]) + shift[i]).astype(jnp.bfloat16)
+            )
+        sums = [contract(parts, held[j]) for j in range(3)]
         q_ref[window, :] = sums[0].astype(q_ref.dtype)
         kv_ref[0, 0, window, :] = sums[1].astype(kv_ref.dtype)
         kv_ref[0, 1, window, :] = sums[2].astype(kv_ref.dtype)
         for s in range(1, frames):
             to_frame(chunk, s).start()
-        return carry
-
-    lax.fori_loop(0, count, step, 0)
+
+    lax.fori_loop(0, count + late, turn, 0)
 
     def finish(chunk, carry):
         relay.drain(chunk)
@@ -289,6 +317,8 @@
         ref = full.at[there, band, :]
         return send(ref, ref, w_send.at[s], w_recv.at[s], head=target_of(me, heads_axis, s))
 
+    sources = [source_of(frame, frames, s) * (rows // BLK) for s in range(frames)]
+
     def tile(t, carry):
         window = pl.ds(pl.multiple_of(t * span, span), span)
         for h in range(heads):
@@ -305,7 +335,7 @@
                 pieces = []
                 new_top = top
                 for block in range(rows // BLK):
-                    row = bias_ref[h, slot, block : block + 1, window]
+                    row = bias_ref[h, pl.ds(sources[slot] + block, 1), window]
                     part = scores[block * BLK : (block + 1) * BLK] * factor + row
                     new_top = jnp.maximum(new_top, jnp.max(part, axis=0, keepdims=True))
                     pieces.append(part)
@@ -326,7 +356,7 @@
 
         @pl.when(t >= 1)
         def _():
-            relay.pass_on(t - 1, 1)
+            relay.advance(t - 1, count)
 
         @pl.when(t == count // 2)
         def _():
@@ -340,29 +370,26 @@
 
     lax.fori_loop(0, count, tile, 0)
 
-    def mix(t, carry):
-        @pl.when(t == count - 1)
-        def _():
-            relay.pass_on(t, 1)
-
-        for distance in range(2, heads_axis // 2):
-            relay.pass_on(t, distance)
+    late = max(heads_axis // 2 - 2, 0)
+
+    def rest(i, carry):
+        relay.advance(i, count)
+        return carry
+
+    lax.fori_loop(count - 1, count + late, rest, 0)
+    for s in range(1, frames):
+        from_frame(s).wait_recv()
+
+    def out(t, carry):
         relay.collect(t)
-
-        @pl.when(t == 0)
-        def _():
-            for s in range(1, frames):
-                from_frame(s).wait_recv()
-
         window = pl.ds(pl.multiple_of(t * span, span), span)
-        total = jnp.zeros(tokens[window, :].shape, jnp.float32)
-        for i in range(heads_axis):
-            total += jnp.dot(done[i, window, :], full[i], preferred_element_type=jnp.float32)
+        weight = full[...].reshape(heads_axis * inner, full.shape[2])
+        total = contract([done[i, window, :] for i in range(heads_axis)], weight)
         wide = tokens[window, :].astype(jnp.float32)
         out_ref[window, :] = (wide + gate[...] * total).astype(out_ref.dtype)
         return carry
 
-    lax.fori_loop(0, count, mix, 0)
+    lax.fori_loop(0, count, out, 0)
 
     def finish(t, carry):
         relay.drain(t)
@@ -419,21 +446,12 @@
     local_rows, local_cols = tokens.shape
     heads_here = block_mask.shape[0]
     head = lax.axis_index("head")
-    frame = lax.axis_index("frame")
     shift = modulation[0].reshape(heads_axis, 1, local_cols)
     gain = modulation[1].reshape(heads_axis, 1, local_cols)
     gate = lax.dynamic_slice_in_dim(modulation[2:3], head * local_cols, local_cols, 1)
 
-    per_frame = local_rows // BLK
     bias = jnp.where(block_mask > 0, 0.0, NEGATIVE).astype(jnp.float32)
-    bias = jnp.stack(
-        [
-            lax.dynamic_slice_in_dim(bias, source_of(frame, frames, s) * per_frame, per_frame, 2)
-            for s in range(frames)
-        ],
-        axis=1,
-    )
-    bias = jnp.repeat(bias.transpose(0, 1, 3, 2), BLK, axis=3)
+    bias = jnp.repeat(bias.transpose(0, 2, 1), BLK, axis=2)
     query, pairs = gather_project(frames, heads_axis, tokens, shift, gain, qkv_weight)
     return attend_mix(
         frames, heads_axis, heads_here, query, pairs, bias, out_weight, tokens, gate

time: 202 us -> 179 us (0.89); the launches traced: 202 us -> 176 us
  Pallas kernels: 196 us -> 169 us
    pallas_call x1, Pallas kernels: 76 us -> 60 us  [attend_mix(): pl.pallas_call(functools.partial(attend_kernel, frames, heads_axis, heads...]
    pallas_call x1, Pallas kernels: 120 us -> 109 us  [gather_project(): pl.pallas_call(functools.partial(gather_kernel, frames, heads_axis, count...]
where the time goes in v2:
time: 179 us; the launch traced here: 176 us
  Pallas kernels  169 us (94%)
  local copies, waits for them, and re-layouts  5.75 us (3%)
    pallas_call x1, Pallas kernels, gather_project(): pl.pallas_call(functools.partial(gather_kernel, frames, heads_axis, count...  109 us
    pallas_call x1, Pallas kernels, attend_mix(): pl.pallas_call(functools.partial(attend_kernel, frames, heads_axis, heads...  60 us

profile of v2, /device:TPU:1, one launch (start us, length us, event | category | flops | bytes accessed | tf_op | source)
XLA Modules:
  0.0 175.9 jit_solution(6857459256087557731)
XLA Ops:
  0.0 0.7 select_bitcast_fusion
  0.7 0.1 copy.6
  0.8 1.7 fusion
  2.5 0.6 constant_dynamic-slice_fusion.gate
  3.1 0.1 broadcast_in_dim.13
  3.2 0.8 reshape.3.bias_ref
  4.0 109.4 %gather_project.1 = (bf16[1024,256]{1,0:T(8,128)(2,1)}, bf16[4,2,1024,256]{3,2,1,0:T(8,128)(2,1)}) custom-call(bf16[1024,640]{1,0:T(8,128)(2,1)} %tokens.3, f32[8,1,640]{2,1,0:T(1,128)} %bitcast.6, f32[8,1,640]{2,1,0:T(1,128)} %bitcast.7, bf16[3,5120,256]{2,1,0:T(8,128)(2,1)} %weight.2), custom_call_target="tpu_custom_call" | custom-call | tf_op jit(solution)/shard_map/gather_project/pallas_call | solution.py:250
  113.4 60.0 %attend_mix.1 = bf16[1024,640]{1,0:T(8,128)(2,1)} custom-call(bf16[1024,256]{1,0:T(8,128)(2,1)} %get-tuple-element.7.q_ref, bf16[4,2,1024,256]{3,2,1,0:T(8,128)(2,1)} %get-tuple-element.8.kv_ref, f32[2,32,1024]{2,1,0:T(8,128)} %reshape.3.bias_ref, bf16[256,5120]{1,0:T(8,128)(2,1)} %weight.3, bf16[1024,640]{1,0:T(8,128)(2,1)} %tokens.3, ...), custom_call_target="tpu_custom_call" | custom-call | tf_op jit(solution)/shard_map/attend_mix/pallas_call | solution.py:422
  173.4 2.5 %copy.8 = bf16[1024,640]{1,0:T(8,128)(2,1)} copy(bf16[1024,640]{1,0:T(8,128)(2,1)} %attend_mix.1) | data formatting | bytes 2621440

commit v3 on v2

--- a/solution.py
+++ b/solution.py
@@ -157,8 +157,9 @@
 
 
 def gather_kernel(
-    frames, heads_axis, count, tokens, shift, gain, weight, q_ref, kv_ref,
-    got, held, far_send, far_recv, pair_send, pair_recv, kv_send, kv_recv, local,
+    frames, heads_axis, count, w_slice, tokens, modulation, weight, out_weight, q_ref, kv_ref,
+    band_ref, got, held, far_send, far_recv, pair_send, pair_recv, kv_send, kv_recv, w_send,
+    w_recv, local,
 ):
     me, frame = lax.axis_index("head"), lax.axis_index("frame")
     rows, cols = tokens.shape
@@ -169,6 +170,10 @@
     load.start()
     mine = pltpu.make_async_copy(tokens, got.at[me], local.at[1])
     mine.start()
+    share = band_ref.shape[1]
+    band = pl.ds(pl.multiple_of(frame * share, share), share)
+    keep = pltpu.make_async_copy(w_slice(out_weight, band, me), band_ref.at[me], local.at[2])
+    keep.start()
     greet(me, frame, heads_axis, frames)
     relay = Relay(me, heads_axis, got, span, (far_send, far_recv, pair_send, pair_recv))
 
@@ -191,10 +196,22 @@
             frame=target_of(frame, frames, s),
         )
 
+    def to_head(s):
+        there = target_of(me, heads_axis, s)
+        return send(
+            w_slice(out_weight, band, there), band_ref.at[me], w_send.at[s], w_recv.at[s],
+            head=there,
+        )
+
     late = max(heads_axis // 2 - 2, 0)
 
     def turn(i, carry):
         relay.advance(i, count)
+
+        @pl.when(i == count + late - 2)
+        def _():
+            for s in range(1, heads_axis):
+                to_head(s).start()
 
         @pl.when(i >= late)
         def _():
@@ -218,8 +235,10 @@
         parts = []
         for i in range(heads_axis):
             wide = got[i, window, :].astype(jnp.float32)
+            shift = modulation[0:1, i * cols : (i + 1) * cols]
+            gain = modulation[1:2, i * cols : (i + 1) * cols]
             parts.append(
-                ((wide - center) * inverse * (1.0 + gain[i]) + shift[i]).astype(jnp.bfloat16)
+                ((wide - center) * inverse * (1.0 + gain) + shift).astype(jnp.bfloat16)
             )
         sums = [contract(parts, held[j]) for j in range(3)]
         q_ref[window, :] = sums[0].astype(q_ref.dtype)
@@ -237,9 +256,15 @@
         return carry
 
     lax.fori_loop(0, count, finish, 0)
-
-
-def gather_project(frames, heads_axis, tokens, shift, gain, weight):
+    keep.wait()
+    for s in range(1, heads_axis):
+        there = source_of(me, heads_axis, s)
+        ref = band_ref.at[there]
+        send(ref, ref, w_send.at[s], w_recv.at[s], head=target_of(me, heads_axis, s)).wait_recv()
+        to_head(s).wait_send()
+
+
+def gather_project(frames, heads_axis, tokens, modulation, weight, out_weight):
     rows, cols = tokens.shape
     inner = weight.shape[2]
     count = TOKEN_CHUNKS
@@ -247,13 +272,23 @@
     whole = pl.BlockSpec(memory_space=pltpu.VMEM)
     away = pl.BlockSpec(memory_space=pl.ANY)
     sem = pltpu.SemaphoreType.DMA
+    if cols % 128 == 0:
+        def w_slice(ref, band, there):
+            return ref.at[band, pl.ds(pl.multiple_of(there * cols, cols), cols)]
+    else:
+        out_weight = out_weight.reshape(inner, heads_axis, cols).transpose(1, 0, 2)
+
+        def w_slice(ref, band, there):
+            return ref.at[there, band, :]
+
     return pl.pallas_call(
-        functools.partial(gather_kernel, frames, heads_axis, count),
-        in_specs=[away, whole, whole, away],
-        out_specs=[whole, whole],
+        functools.partial(gather_kernel, frames, heads_axis, count, w_slice),
+        in_specs=[away, whole, away, away],
+        out_specs=[whole, whole, whole],
         out_shape=[
             jax.ShapeDtypeStruct((rows, inner), jnp.bfloat16),
             jax.ShapeDtypeStruct((frames, 2, rows, inner), jnp.bfloat16),
+            jax.ShapeDtypeStruct((heads_axis, inner // frames, cols), jnp.bfloat16),
         ],
         scratch_shapes=[
             pltpu.VMEM((heads_axis, rows, cols), jnp.bfloat16),
@@ -264,17 +299,18 @@
             sem((line, count)),
             sem((count, frames)),
             sem((count, frames)),
-            sem((2,)),
+            sem((heads_axis,)),
+            sem((heads_axis,)),
+            sem((3,)),
         ],
         compiler_params=pltpu.CompilerParams(collective_id=0, has_side_effects=True),
         name="gather_project",
-    )(tokens, shift, gain, weight)
+    )(tokens, modulation, weight, out_weight)
 
 
 def attend_kernel(
-    frames, heads_axis, heads, count, w_slice, q_ref, kv_ref, bias_ref, weight, tokens, gate,
-    out_ref, done, full, far_send, far_recv, pair_send, pair_recv, w_send, w_recv, x_send,
-    x_recv, local,
+    frames, heads_axis, heads, count, q_ref, kv_ref, bias_ref, band_ref, tokens, gate,
+    out_ref, done, full, far_send, far_recv, pair_send, pair_recv, x_send, x_recv, local,
 ):
     me, frame = lax.axis_index("head"), lax.axis_index("frame")
     rows, inner = q_ref.shape
@@ -286,21 +322,12 @@
     relay = Relay(me, heads_axis, done, span, (far_send, far_recv, pair_send, pair_recv))
     band = pl.ds(pl.multiple_of(frame * share, share), share)
 
-    def to_head(s):
-        there = target_of(me, heads_axis, s)
-        return send(
-            w_slice(weight, band, there), full.at[me, band, :], w_send.at[s], w_recv.at[s],
-            head=there,
-        )
-
-    keep = pltpu.make_async_copy(w_slice(weight, band, me), full.at[me, band, :], local.at[0])
+    keep = pltpu.make_async_copy(band_ref, full.at[:, band, :], local.at[0])
     keep.start()
-    for s in range(1, heads_axis):
-        to_head(s).start()
 
     def to_frame(s):
         return send(
-            full.at[:, band, :], full.at[:, band, :], x_send.at[s], x_recv.at[s],
+            band_ref, full.at[:, band, :], x_send.at[s], x_recv.at[s],
             frame=target_of(frame, frames, s),
         )
 
@@ -312,11 +339,8 @@
             frame=target_of(frame, frames, s),
         )
 
-    def from_head(s):
-        there = source_of(me, heads_axis, s)
-        ref = full.at[there, band, :]
-        return send(ref, ref, w_send.at[s], w_recv.at[s], head=target_of(me, heads_axis, s))
-
+    for s in range(1, frames):
+        to_frame(s).start()
     sources = [source_of(frame, frames, s) * (rows // BLK) for s in range(frames)]
 
     def tile(t, carry):
@@ -358,14 +382,6 @@
         def _():
             relay.advance(t - 1, count)
 
-        @pl.when(t == count // 2)
-        def _():
-            keep.wait()
-            for s in range(1, heads_axis):
-                from_head(s).wait_recv()
-            for s in range(1, frames):
-                to_frame(s).start()
-
         return carry
 
     lax.fori_loop(0, count, tile, 0)
@@ -376,11 +392,16 @@
         relay.advance(i, count)
         return carry
 
-    lax.fori_loop(count - 1, count + late, rest, 0)
+    lax.fori_loop(count - 1, count + late - 1, rest, 0)
+    keep.wait()
     for s in range(1, frames):
         from_frame(s).wait_recv()
 
     def out(t, carry):
+        @pl.when(t == count - 1)
+        def _():
+            relay.advance(count + late - 1, count)
+
         relay.collect(t)
         window = pl.ds(pl.multiple_of(t * span, span), span)
         weight = full[...].reshape(heads_axis * inner, full.shape[2])
@@ -396,13 +417,11 @@
         return carry
 
     lax.fori_loop(0, count, finish, 0)
-    for s in range(1, heads_axis):
-        to_head(s).wait_send()
     for s in range(1, frames):
         to_frame(s).wait_send()
 
 
-def attend_mix(frames, heads_axis, heads, query, pairs, bias, out_weight, tokens, gate):
+def attend_mix(frames, heads_axis, heads, query, pairs, bias, band, tokens, gate):
     rows, inner = query.shape
     cols = tokens.shape[1]
     count = QUERY_CHUNKS
@@ -410,18 +429,9 @@
     whole = pl.BlockSpec(memory_space=pltpu.VMEM)
     away = pl.BlockSpec(memory_space=pl.ANY)
     sem = pltpu.SemaphoreType.DMA
-    if cols % 128 == 0:
-        def w_slice(ref, band, there):
-            return ref.at[band, pl.ds(pl.multiple_of(there * cols, cols), cols)]
-    else:
-        out_weight = out_weight.reshape(inner, heads_axis, cols).transpose(1, 0, 2)
-
-        def w_slice(ref, band, there):
-            return ref.at[there, band, :]
-
     return pl.pallas_call(
-        functools.partial(attend_kernel, frames, heads_axis, heads, count, w_slice),
-        in_specs=[whole, whole, whole, away, whole, whole],
+        functools.partial(attend_kernel, frames, heads_axis, heads, count),
+        in_specs=[whole] * 6,
         out_specs=whole,
         out_shape=jax.ShapeDtypeStruct((rows, cols), jnp.bfloat16),
         scratch_shapes=[
@@ -431,31 +441,27 @@
             sem((line, count)),
             sem((line, count)),
             sem((line, count)),
-            sem((heads_axis,)),
-            sem((heads_axis,)),
             sem((frames,)),
             sem((frames,)),
             sem((1,)),
         ],
         compiler_params=pltpu.CompilerParams(collective_id=1, has_side_effects=True),
         name="attend_mix",
-    )(query, pairs, bias, out_weight, tokens, gate)
+    )(query, pairs, bias, band, tokens, gate)
 
 
 def shards(frames, heads_axis, tokens, qkv_weight, out_weight, modulation, block_mask):
     local_rows, local_cols = tokens.shape
     heads_here = block_mask.shape[0]
     head = lax.axis_index("head")
-    shift = modulation[0].reshape(heads_axis, 1, local_cols)
-    gain = modulation[1].reshape(heads_axis, 1, local_cols)
     gate = lax.dynamic_slice_in_dim(modulation[2:3], head * local_cols, local_cols, 1)
 
     bias = jnp.where(block_mask > 0, 0.0, NEGATIVE).astype(jnp.float32)
     bias = jnp.repeat(bias.transpose(0, 2, 1), BLK, axis=2)
-    query, pairs = gather_project(frames, heads_axis, tokens, shift, gain, qkv_weight)
-    return attend_mix(
-        frames, heads_axis, heads_here, query, pairs, bias, out_weight, tokens, gate
+    query, pairs, band = gather_project(
+        frames, heads_axis, tokens, modulation, qkv_weight, out_weight
     )
+    return attend_mix(frames, heads_axis, heads_here, query, pairs, bias, band, tokens, gate)
 
 
 def solution(mesh):

time: 179 us -> 173 us (0.966); the launches traced: 176 us -> 173 us
  Pallas kernels: 169 us -> 167 us
    pallas_call x1, Pallas kernels: 60 us -> 53.7 us  [attend_mix(): pl.pallas_call(functools.partial(attend_kernel, frames, heads_axis, heads...]
    pallas_call x1, Pallas kernels: 109 us -> 113 us  [gather_project(): pl.pallas_call(functools.partial(gather_kernel, frames, heads_axis, count...]
where the time goes in v3:
time: 173 us
  Pallas kernels  167 us (97%)
  local copies, waits for them, and re-layouts  4.94 us (3%)
    pallas_call x1, Pallas kernels, gather_project(): pl.pallas_call(functools.partial(gather_kernel, frames, heads_axis, count...  113 us
    pallas_call x1, Pallas kernels, attend_mix(): pl.pallas_call(functools.partial(attend_kernel, frames, heads_axis, heads...  53.7 us

profile of v3, /device:TPU:1, one launch (start us, length us, event | category | flops | bytes accessed | tf_op | source)
XLA Modules:
  0.0 172.8 jit_solution(17517800441336159020)
XLA Ops:
  0.0 0.7 select_bitcast_fusion
  0.7 0.9 slice.3
  1.6 0.6 constant_dynamic-slice_fusion.gate
  2.2 0.1 copy.6
  2.3 0.1 broadcast_in_dim.13
  2.4 0.8 reshape.3.bias_ref
  3.2 113.5 %gather_project.1 = (bf16[1024,256]{1,0:T(8,128)(2,1)}, bf16[4,2,1024,256]{3,2,1,0:T(8,128)(2,1)}, bf16[8,64,640]{2,1,0:T(8,128)(2,1)}) custom-call(bf16[1024,640]{1,0:T(8,128)(2,1)} %tokens.3, f32[3,5120]{1,0:T(4,128)} %modulation.1, bf16[3,5120,256]{2,1,0:T(8,128)(2,1)} %weight.1, bf16[256,5120]{1,0:T(8,128)(2,1)} %out_weight.1), custom_call_target="tpu_custom_call" | custom-call | tf_op jit(solution)/shard_map/gather_project/pallas_call | solution.py:284
  116.6 53.7 %attend_mix.1 = bf16[1024,640]{1,0:T(8,128)(2,1)} custom-call(bf16[1024,256]{1,0:T(8,128)(2,1)} %get-tuple-element.8.q_ref, bf16[4,2,1024,256]{3,2,1,0:T(8,128)(2,1)} %get-tuple-element.9.kv_ref, f32[2,32,1024]{2,1,0:T(8,128)} %reshape.3.bias_ref, bf16[8,64,640]{2,1,0:T(8,128)(2,1)} %get-tuple-element.10.band_ref, bf16[1024,640]{1,0:T(8,128)(2,1)} %tokens.3, ...), custom_call_target="tpu_custom_call" | custom-call | tf_op jit(solution)/shard_map/attend_mix/pallas_call | solution.py:432
  170.3 2.5 %copy.8 = bf16[1024,640]{1,0:T(8,128)(2,1)} copy(bf16[1024,640]{1,0:T(8,128)(2,1)} %attend_mix.1) | data formatting | bytes 2621440

commit v4 on v3

--- a/solution.py
+++ b/solution.py
@@ -309,7 +309,7 @@
 
 
 def attend_kernel(
-    frames, heads_axis, heads, count, q_ref, kv_ref, bias_ref, band_ref, tokens, gate,
+    frames, heads_axis, heads, count, q_ref, kv_ref, mask_ref, band_ref, tokens, gate,
     out_ref, done, full, far_send, far_recv, pair_send, pair_recv, x_send, x_recv, local,
 ):
     me, frame = lax.axis_index("head"), lax.axis_index("frame")
@@ -342,6 +342,8 @@
     for s in range(1, frames):
         to_frame(s).start()
     sources = [source_of(frame, frames, s) * (rows // BLK) for s in range(frames)]
+
+    wide = span // BLK
 
     def tile(t, carry):
         window = pl.ds(pl.multiple_of(t * span, span), span)
@@ -359,7 +361,21 @@
                 pieces = []
                 new_top = top
                 for block in range(rows // BLK):
-                    row = bias_ref[h, pl.ds(sources[slot] + block, 1), window]
+                    row = jnp.concatenate(
+                        [
+                            jnp.full(
+                                (1, BLK),
+                                jnp.where(
+                                    mask_ref[h, t * wide + k, sources[slot] + block] > 0,
+                                    0.0,
+                                    NEGATIVE,
+                                ),
+                                jnp.float32,
+                            )
+                            for k in range(wide)
+                        ],
+                        axis=1,
+                    )
                     part = scores[block * BLK : (block + 1) * BLK] * factor + row
                     new_top = jnp.maximum(new_top, jnp.max(part, axis=0, keepdims=True))
                     pieces.append(part)
@@ -406,8 +422,13 @@
         window = pl.ds(pl.multiple_of(t * span, span), span)
         weight = full[...].reshape(heads_axis * inner, full.shape[2])
         total = contract([done[i, window, :] for i in range(heads_axis)], weight)
-        wide = tokens[window, :].astype(jnp.float32)
-        out_ref[window, :] = (wide + gate[...] * total).astype(out_ref.dtype)
+        if gate.shape[1] == out_ref.shape[1]:
+            own = gate[...]
+        else:
+            cols = out_ref.shape[1]
+            own = gate[2:3, pl.ds(pl.multiple_of(me * cols, cols), cols)]
+        held = tokens[window, :].astype(jnp.float32)
+        out_ref[window, :] = (held + own * total).astype(out_ref.dtype)
         return carry
 
     lax.fori_loop(0, count, out, 0)
@@ -421,7 +442,7 @@
         to_frame(s).wait_send()
 
 
-def attend_mix(frames, heads_axis, heads, query, pairs, bias, band, tokens, gate):
+def attend_mix(frames, heads_axis, heads, query, pairs, mask, band, tokens, gate):
     rows, inner = query.shape
     cols = tokens.shape[1]
     count = QUERY_CHUNKS
@@ -431,7 +452,7 @@
     sem = pltpu.SemaphoreType.DMA
     return pl.pallas_call(
         functools.partial(attend_kernel, frames, heads_axis, heads, count),
-        in_specs=[whole] * 6,
+        in_specs=[whole, whole, pl.BlockSpec(memory_space=pltpu.SMEM), whole, whole, whole],
         out_specs=whole,
         out_shape=jax.ShapeDtypeStruct((rows, cols), jnp.bfloat16),
         scratch_shapes=[
@@ -447,21 +468,21 @@
         ],
         compiler_params=pltpu.CompilerParams(collective_id=1, has_side_effects=True),
         name="attend_mix",
-    )(query, pairs, bias, band, tokens, gate)
+    )(query, pairs, mask, band, tokens, gate)
 
 
 def shards(frames, heads_axis, tokens, qkv_weight, out_weight, modulation, block_mask):
     local_rows, local_cols = tokens.shape
     heads_here = block_mask.shape[0]
     head = lax.axis_index("head")
-    gate = lax.dynamic_slice_in_dim(modulation[2:3], head * local_cols, local_cols, 1)
-
-    bias = jnp.where(block_mask > 0, 0.0, NEGATIVE).astype(jnp.float32)
-    bias = jnp.repeat(bias.transpose(0, 2, 1), BLK, axis=2)
+    gate = modulation
+    if local_cols % 128:
+        gate = lax.dynamic_slice_in_dim(modulation[2:3], head * local_cols, local_cols, 1)
+
     query, pairs, band = gather_project(
         frames, heads_axis, tokens, modulation, qkv_weight, out_weight
     )
-    return attend_mix(frames, heads_axis, heads_here, query, pairs, bias, band, tokens, gate)
+    return attend_mix(frames, heads_axis, heads_here, query, pairs, block_mask, band, tokens, gate)
 
 
 def solution(mesh):

time: 173 us -> 170 us (0.983)
  local copies, waits for them, and re-layouts: 4.94 us -> 2.49 us
where the time goes in v4:
time: 170 us
  Pallas kernels  167 us (98%)
  local copies, waits for them, and re-layouts  2.49 us (1%)
    pallas_call x1, Pallas kernels, gather_project(): pl.pallas_call(functools.partial(gather_kernel, frames, heads_axis, count...  113 us
    pallas_call x1, Pallas kernels, attend_mix(): pl.pallas_call(functools.partial(attend_kernel, frames, heads_axis, heads...  53.6 us

profile of v4, /device:TPU:1, one launch (start us, length us, event | category | flops | bytes accessed | tf_op | source)
XLA Modules:
  0.0 169.6 jit_solution(16055482849477712611)
XLA Ops:
  0.0 113.5 %gather_project.1 = (bf16[1024,256]{1,0:T(8,128)(2,1)}, bf16[4,2,1024,256]{3,2,1,0:T(8,128)(2,1)}, bf16[8,64,640]{2,1,0:T(8,128)(2,1)}) custom-call(bf16[1024,640]{1,0:T(8,128)(2,1)} %tokens.3, f32[3,5120]{1,0:T(4,128)} %gate.1, bf16[3,5120,256]{2,1,0:T(8,128)(2,1)} %weight.1, bf16[256,5120]{1,0:T(8,128)(2,1)} %out_weight.1), custom_call_target="tpu_custom_call" | custom-call | tf_op jit(solution)/shard_map/gather_project/pallas_call | solution.py:284
  113.5 53.6 %attend_mix.1 = bf16[1024,640]{1,0:T(8,128)(2,1)} custom-call(bf16[1024,256]{1,0:T(8,128)(2,1)} %get-tuple-element.8.q_ref, bf16[4,2,1024,256]{3,2,1,0:T(8,128)(2,1)} %get-tuple-element.9.kv_ref, s32[2,8,32]{2,1,0:T(8,128)} %mask_ref.1, bf16[8,64,640]{2,1,0:T(8,128)(2,1)} %get-tuple-element.10.band_ref, bf16[1024,640]{1,0:T(8,128)(2,1)} %tokens.3, ...), custom_call_target="tpu_custom_call" | custom-call | tf_op jit(solution)/shard_map/attend_mix/pallas_call | solution.py:453
  167.1 2.5 %copy.7 = bf16[1024,640]{1,0:T(8,128)(2,1)} copy(bf16[1024,640]{1,0:T(8,128)(2,1)} %attend_mix.1) | data formatting | bytes 2621440

commit v5 on v4

--- a/solution.py
+++ b/solution.py
@@ -13,7 +13,7 @@
 EPSILON = 1e-06
 LOG2E = math.log2(math.e)
 TOKEN_CHUNKS = 8
-QUERY_CHUNKS = 4
+QUERY_CHUNKS = 8
 
 
 def source_of(me, size, step):

time: 170 us -> 167 us (0.982)
  Pallas kernels: 167 us -> 165 us
    pallas_call x1, Pallas kernels: 53.6 us -> 51.3 us  [attend_mix(): pl.pallas_call(functools.partial(attend_kernel, frames, heads_axis, heads...]
where the time goes in v5:
time: 167 us
  Pallas kernels  165 us (99%)
  local copies, waits for them, and re-layouts  2.49 us (1%)
    pallas_call x1, Pallas kernels, gather_project(): pl.pallas_call(functools.partial(gather_kernel, frames, heads_axis, count...  113 us
    pallas_call x1, Pallas kernels, attend_mix(): pl.pallas_call(functools.partial(attend_kernel, frames, heads_axis, heads...  51.3 us

profile of v5, /device:TPU:1, one launch (start us, length us, event | category | flops | bytes accessed | tf_op | source)
XLA Modules:
  0.0 167.2 jit_solution(15706429761399980481)
XLA Ops:
  0.0 113.5 %gather_project.1 = (bf16[1024,256]{1,0:T(8,128)(2,1)}, bf16[4,2,1024,256]{3,2,1,0:T(8,128)(2,1)}, bf16[8,64,640]{2,1,0:T(8,128)(2,1)}) custom-call(bf16[1024,640]{1,0:T(8,128)(2,1)} %tokens.3, f32[3,5120]{1,0:T(4,128)} %gate.1, bf16[3,5120,256]{2,1,0:T(8,128)(2,1)} %weight.1, bf16[256,5120]{1,0:T(8,128)(2,1)} %out_weight.1), custom_call_target="tpu_custom_call" | custom-call | tf_op jit(solution)/shard_map/gather_project/pallas_call | solution.py:284
  113.5 51.3 %attend_mix.1 = bf16[1024,640]{1,0:T(8,128)(2,1)} custom-call(bf16[1024,256]{1,0:T(8,128)(2,1)} %get-tuple-element.8.q_ref, bf16[4,2,1024,256]{3,2,1,0:T(8,128)(2,1)} %get-tuple-element.9.kv_ref, s32[2,8,32]{2,1,0:T(8,128)} %mask_ref.1, bf16[8,64,640]{2,1,0:T(8,128)(2,1)} %get-tuple-element.10.band_ref, bf16[1024,640]{1,0:T(8,128)(2,1)} %tokens.3, ...), custom_call_target="tpu_custom_call" | custom-call | tf_op jit(solution)/shard_map/attend_mix/pallas_call | solution.py:453
  164.8 2.5 %copy.7 = bf16[1024,640]{1,0:T(8,128)(2,1)} copy(bf16[1024,640]{1,0:T(8,128)(2,1)} %attend_mix.1) | data formatting | bytes 2621440
